TPU v7x, 32 devices: a whole 2x2x4 slice. The times are simulated.
32 devices in a mesh: gx: 16 (over z, y, core), gy: 2 (over x).
Axes of the slice: x: 2, y: 2, z: 4, core: 2. Of those that a mesh axis runs over, the one named last changes fastest.
Arguments:
- loads: float32 [8, 2, 16384], P(None, 'gy', 'gx'), may hold values from -6 to 6
- dual_op: bfloat16 [2, 16384, 1024], P('gy', 'gx')
- iface: int32 [2, 16, 1024], P('gy', 'gx'), may hold values from 0 to 1023, each once within a row
- precond: float32 [2, 16384], P('gy', 'gx'), may hold values from 0.3 to 3
- corner_map: float32 [2, 128, 16384], P('gy', None, 'gx'), may hold values from -0.25 to 0.25
- coarse_inv: float32 [128, 128], replicated
- elem_stiff: float32 [8, 8], replicated
- elem_dofs: int32 [8, 1024, 256], P(None, 'gx', 'gy'), may hold values from 0 to 1023
- density: float32 [1024, 256], P('gx', 'gy'), may hold values from 0.1 to 1
- passive: int32 [1024, 256], P('gx', 'gy'), may hold values 0 or 1
Outputs:
- adjoint: float32 [8, 2, 16384], P(None, 'gy', 'gx')
- sens: float32 [1024, 256], P('gx', 'gy')
All inputs are finite; a program needn't handle non-finite values. No bound on the sum of `passive` on one device may be relied on, other than what follows from the above.
Results may differ from a plain program's by a relative error of at most 0.00052.
Values sent between devices are 32-bit elements; how exact they have to be, the bound alone decides.
No kernel may reach another device: no remote copies, remote signals or barrier semaphores. Data moves between devices by JAX's collectives and lax.ppermute only.
A program may use at most 128 MiB of HBM per device.

v0:
```python
import jax
import jax.numpy as jnp
from jax import lax
from jax.sharding import PartitionSpec as P

R = 128
ITERS = 2
SWEEPS = 3
coupling = 0.3
radius_sq = 2.0
penalty = 3.0


def padded_2(array, sides, width):
    for axis, dim in sides:
        size, length = (lax.axis_size(axis), array.shape[dim])
        up = [(i, (i + 1) % size) for i in range(size - 1)]
        down = [(j, i) for i, j in up]
        last = lax.slice_in_dim(array, length - width, length, axis=dim)
        leading = lax.slice_in_dim(array, 0, width, axis=dim)
        before = lax.ppermute(last, axis, up)
        after = lax.ppermute(leading, axis, down)
        array = jnp.concatenate([before, array, after], axis=dim)
    return array


def local_part(vec, op_local, left_idx, right_idx):
    local = jnp.einsum(
        "ck,mk->cm", vec.astype(jnp.bfloat16), op_local, preferred_element_type=jnp.float32
    )
    width = left_idx.shape[0]
    outgoing = jnp.concatenate([vec[:, left_idx], vec[:, right_idx]], axis=1)
    extended = padded_2(outgoing, (("gx", 1),), width)
    local = local.at[:, left_idx].add(-coupling * extended[:, :width])
    local = local.at[:, right_idx].add(-coupling * extended[:, 3 * width :])
    return local


def apply_dual(vec, op_local, left_idx, right_idx, corners, coarse_inv):
    hi = lax.Precision.HIGHEST
    local = local_part(vec, op_local, left_idx, right_idx)
    csum = lax.psum(jnp.dot(vec, corners.T, precision=hi), ("gx", "gy"))
    coarse_vals = jnp.dot(csum, coarse_inv.T, precision=hi)
    return local + jnp.dot(coarse_vals, corners, precision=hi)


def inner(first, second):
    return jnp.sum(first * second, axis=1)[:, None]


def residual_products(resid, zvec):
    return lax.psum(inner(resid, zvec), ("gx", "gy"))


def on_device(
    loads, dual_op, iface, precond, corner_map, coarse_inv, elem_stiff, elem_dofs, density, passive
):
    hi = lax.Precision.HIGHEST
    op_local = dual_op[0]
    width = R
    left_idx = iface[0, 0, :width]
    right_idx = iface[0, 0, width : 2 * width]
    corners = corner_map[0]
    scaling = precond[0][None, :]
    resid = loads[:, 0, :]
    adjoint = jnp.zeros_like(resid)
    zvec = scaling * resid
    direction = zvec
    rz_now = residual_products(resid, zvec)
    for step in range(ITERS):
        image = apply_dual(direction, op_local, left_idx, right_idx, corners, coarse_inv)
        alpha = rz_now / lax.psum(inner(direction, image), ("gx", "gy"))
        adjoint = adjoint + alpha * direction
        resid = resid - alpha * image
        if step + 1 < ITERS:
            zvec = scaling * resid
            rz_next = residual_products(resid, zvec)
            direction = zvec + rz_next / rz_now * direction
            rz_now = rz_next
    nodal = adjoint[:, elem_dofs]
    pushed = jnp.einsum("ab,cbxy->caxy", elem_stiff, nodal, precision=hi)
    energy = jnp.sum(nodal * pushed, axis=(0, 1))
    grad = jnp.where(passive == 1, 0.0, -penalty * density * density * energy)
    diag = 1.0 + 4.0 * radius_sq
    smooth = grad / diag
    for sweep in range(SWEEPS - 1):
        padded = padded_2(smooth, (("gx", 0), ("gy", 1)), 1)
        beside = padded[2:, 1:-1] + padded[:-2, 1:-1] + padded[1:-1, 2:] + padded[1:-1, :-2]
        smooth = (grad + radius_sq * beside) / diag
    return (adjoint[:, None, :], smooth)


def solution(mesh):
    placed = (
        P(None, "gy", "gx"),
        P("gy", "gx", None),
        P("gy", "gx", None),
        P("gy", "gx"),
        P("gy", None, "gx"),
        P(),
        P(),
        P(None, "gx", "gy"),
        P("gx", "gy"),
        P("gx", "gy"),
    )
    return jax.shard_map(
        on_device,
        mesh=mesh,
        in_specs=placed,
        out_specs=(P(None, "gy", "gx"), P("gx", "gy")),
        check_vma=False,
    )
```

profile of v0, /device:TPU:7, one launch (start us, length us, event | category | flops | bytes accessed | tf_op | source)
XLA Modules:
  0.0 517.5 jit_solution(12681567802003912632)
XLA Ops:
  2.5 1.7 bitcast_multiply_fusion.2
  4.2 2.3 gather_fusion
  6.5 3.7 collective-permute-start
  10.2 2.3 gather_fusion.1
  12.5 1.9 collective-permute-start.1
  15.7 39.5 %psum.43 = f32[8,128]{1,0:T(8,128)S(1)} all-reduce(f32[8,128]{1,0:T(8,128)S(1)} %fusion.22), channel_id=1, replica_groups=mesh['gx'=16,'gy'=2] {'gx','gy'}, use_global_device_ids=true, to_apply=%region_2.0 | all-reduce | flops 1024 | bytes 8192 | tf_op jit(solution)/shard_map/psum | solution.py:42
  56.8 1.8 scatter_custom_fusion
  58.6 1.8 scatter_custom_fusion.1
  60.6 41.0 %all-reduce = (f32[8,1]{0,1:T(1,128)S(1)}, f32[8,1]{0,1:T(1,128)S(1)}) all-reduce(f32[8,1]{0,1:T(1,128)S(1)} %bitcast.112, f32[8,1]{0,1:T(1,128)S(1)} %bitcast.111), channel_id=1, replica_groups=mesh['gx'=16,'gy'=2] {'gx','gy'}, use_global_device_ids=true, to_apply=%region_1.0 | all-reduce | flops 16 | bytes 128 | tf_op jit(solution)/shard_map/psum | solution.py:52
  101.8 39.1 %psum.45 = f32[8,1]{0,1:T(1,128)S(1)} all-reduce(f32[8,1]{0,1:T(1,128)S(1)} %bitcast.113), channel_id=1, replica_groups=mesh['gx'=16,'gy'=2] {'gx','gy'}, use_global_device_ids=true, to_apply=%region_8.0 | all-reduce | flops 8 | bytes 64 | tf_op jit(solution)/shard_map/psum | solution.py:52
  142.3 2.2 fusion.18
  146.9 41.0 %psum.46 = f32[8,128]{1,0:T(8,128)S(1)} all-reduce(f32[8,128]{1,0:T(8,128)S(1)} %fusion.18), channel_id=1, replica_groups=mesh['gx'=16,'gy'=2] {'gx','gy'}, use_global_device_ids=true, to_apply=%region_9.0 | all-reduce | flops 1024 | bytes 8192 | tf_op jit(solution)/shard_map/psum | solution.py:42
  188.1 1.5 fusion.16
  189.5 4.1 collective-permute-start.2
  193.6 1.9 collective-permute-start.3
  197.2 3.3 scatter_custom_fusion.2
  200.6 3.1 scatter_custom_fusion.3
  204.9 38.9 %psum.47 = f32[8,1]{0,1:T(1,128)S(1)} all-reduce(f32[8,1]{0,1:T(1,128)S(1)} %bitcast.114), channel_id=1, replica_groups=mesh['gx'=16,'gy'=2] {'gx','gy'}, use_global_device_ids=true, to_apply=%region_13.0 | all-reduce | flops 8 | bytes 64 | tf_op jit(solution)/shard_map/psum | solution.py:72
  245.1 215.5 %gather_fusion.4 = f32[65536,8]{1,0:T(8,128)} fusion(f32[8,1024]{0,1:T(8,128)S(1)} %multiply_add_fusion.1, s32[65536]{0:T(1024)S(1)} %broadcast_clamp_fusion), kind=kCustom, calls=%fused_computation.4 | custom fusion | bytes 4456448 | tf_op jit(solution)/shard_map/gather | solution.py:80
  460.6 18.7 %copy.20 = f32[8,64,128,8]{2,0,1,3:T(8,128)} copy(f32[8,64,128,8]{3,2,1,0:T(8,128)} %bitcast.103) | data formatting | bytes 4194304 | tf_op jit(solution)/shard_map/gather | solution.py:80
  479.2 4.2 fusion
  483.5 5.7 %collective-permute-start.5 = (f32[1,128]{1,0:T(1,128)S(1)}, f32[1,128]{1,0:T(1,128)S(1)}, u32[]{:S(2)}, u32[]{:S(2)}) collective-permute-start(f32[1,128]{1,0:T(1,128)S(1)} %get-tuple-element.20), channel_id=1, source_target_pairs={{0,2},{2,4},{4,6},{6,8},{8,10},{10,12},{12,14},{14,16},{16,18},{18... | collective-permute-start | bytes 1544 | tf_op jit(solution)/shard_map/ppermute | solution.py:21
  489.2 1.9 collective-permute-start.4
  491.2 3.8 collective-permute-done.4
  495.1 1.4 collective-permute-start.6
  496.5 1.3 collective-permute-start.7
  497.8 3.4 collective-permute-done.7
  501.3 3.6 collective-permute-start.9
  504.9 1.9 collective-permute-start.8
  506.9 3.8 collective-permute-done.8
  512.1 1.3 collective-permute-start.11
  514.2 2.6 collective-permute-done.11
  (72 shorter events, 16.3 us)
Async XLA Ops:
  0.6 55.3 %copy-start = (bf16[1,1024,1024]{2,1,0:T(8,128)(2,1)S(1)}, bf16[1,1024,1024]{2,1,0:T(8,128)(2,1)}, u32[]{:S(2)}) copy-start(bf16[1,1024,1024]{2,1,0:T(8,128)(2,1)} %param.11) | copy-start | bytes 6291460
  0.6 14.6 %copy-start.2 = (f32[1,128,1024]{2,1,0:T(8,128)S(1)}, f32[1,128,1024]{2,1,0:T(8,128)}, u32[]{:S(2)}) copy-start(f32[1,128,1024]{2,1,0:T(8,128)} %param.14) | copy-start | bytes 1572868
  0.7 54.6 %copy-start.4 = (f32[128,128]{1,0:T(8,128)S(1)}, f32[128,128]{1,0:T(8,128)}, u32[]{:S(2)}) copy-start(f32[128,128]{1,0:T(8,128)} %param.15) | copy-start | bytes 196612
  0.7 55.1 %copy-start.5 = (s32[8,64,128]{2,1,0:T(8,128)S(1)}, s32[8,64,128]{2,1,0:T(8,128)}, u32[]{:S(2)}) copy-start(s32[8,64,128]{2,1,0:T(8,128)} %param.17) | copy-start | bytes 786436
  1.5 13.7 %copy-start.11 = (s32[128]{0:T(128)}, s32[128]{0:T(128)S(1)}, u32[]{:S(2)}) copy-start(s32[128]{0:T(128)S(1)} %get-tuple-element.23) | copy-start | bytes 1540
  1.5 57.1 %copy-start.10 = (s32[128]{0:T(128)}, s32[128]{0:T(128)S(1)}, u32[]{:S(2)}) copy-start(s32[128]{0:T(128)S(1)} %get-tuple-element.22) | copy-start | bytes 1540
  6.5 50.3 %collective-permute-start = (f32[8,128]{0,1:T(8,128)}, f32[8,128]{0,1:T(8,128)}, u32[]{:S(2)}, u32[]{:S(2)}) collective-permute-start(f32[8,128]{0,1:T(8,128)} %bitcast.9), channel_id=1, source_target_pairs={{0,2},{2,4},{4,6},{6,8},{8,10},{10,12},{12,14},{14,16},{16,18},{18... | collective-permute-start | bytes 12296 | tf_op jit(solution)/shard_map/ppermute | solution.py:21
  12.5 46.1 %collective-permute-start.1 = (f32[8,128]{0,1:T(8,128)}, f32[8,128]{0,1:T(8,128)}, u32[]{:S(2)}, u32[]{:S(2)}) collective-permute-start(f32[8,128]{0,1:T(8,128)} %bitcast.11), channel_id=1, source_target_pairs={{2,0},{4,2},{6,4},{8,6},{10,8},{12,10},{14,12},{16,14},{18,16},{20... | collective-permute-start | bytes 12296 | tf_op jit(solution)/shard_map/ppermute | solution.py:22
  55.8 4.5 copy-start.6
  60.4 80.6 %copy-start.3 = (f32[8,1024]{0,1:T(8,128)}, f32[8,1024]{0,1:T(8,128)S(1)}, u32[]{:S(2)}) copy-start(f32[8,1024]{0,1:T(8,128)S(1)} %scatter_custom_fusion.1) | copy-start | bytes 98308
  141.0 4.7 copy-start.12
  142.3 61.4 %copy-start.1 = (f32[8,1024]{0,1:T(8,128)}, f32[8,1024]{0,1:T(8,128)S(1)}, u32[]{:S(2)}) copy-start(f32[8,1024]{0,1:T(8,128)S(1)} %multiply_add_fusion) | copy-start | bytes 98308
  189.5 7.7 %collective-permute-start.2 = (f32[8,128]{0,1:T(8,128)}, f32[8,128]{0,1:T(8,128)}, u32[]{:S(2)}, u32[]{:S(2)}) collective-permute-start(f32[8,128]{0,1:T(8,128)} %bitcast.116), channel_id=1, source_target_pairs={{0,2},{2,4},{4,6},{6,8},{8,10},{10,12},{12,14},{14,16},{16,18},{18... | collective-permute-start | bytes 12296 | tf_op jit(solution)/shard_map/ppermute | solution.py:21
  193.6 50.2 %copy-start.13 = (f32[8,1]{0,1:T(1,128)S(1)}, f32[8,1]{0,1:T(1,128)}, u32[]{:S(2)}) copy-start(f32[8,1]{0,1:T(1,128)} %copy-done.12) | copy-start | bytes 100
  193.6 6.9 %collective-permute-start.3 = (f32[8,128]{0,1:T(8,128)}, f32[8,128]{0,1:T(8,128)S(1)}, u32[]{:S(2)}, u32[]{:S(2)}) collective-permute-start(f32[8,128]{0,1:T(8,128)} %bitcast.115), channel_id=1, source_target_pairs={{2,0},{4,2},{6,4},{8,6},{10,8},{12,10},{14,12},{16,14},{18,16},{20... | collective-permute-start | bytes 12296 | tf_op jit(solution)/shard_map/ppermute | solution.py:22
  460.6 18.7 %copy-start.9 = (f32[8,8]{1,0:T(8,128)S(1)}, f32[8,8]{1,0:T(8,128)}, u32[]{:S(2)}) copy-start(f32[8,8]{1,0:T(8,128)} %param.16) | copy-start | bytes 772
  479.2 4.3 copy-start.7
  479.2 4.3 copy-start.8
  483.5 7.6 %collective-permute-start.5 = (f32[1,128]{1,0:T(1,128)S(1)}, f32[1,128]{1,0:T(1,128)S(1)}, u32[]{:S(2)}, u32[]{:S(2)}) collective-permute-start(f32[1,128]{1,0:T(1,128)S(1)} %get-tuple-element.20), channel_id=1, source_target_pairs={{0,2},{2,4},{4,6},{6,8},{8,10},{10,12},{12,14},{14,16},{16,18},{18... | collective-permute-start | bytes 1544 | tf_op jit(solution)/shard_map/ppermute | solution.py:21
  489.2 5.8 %collective-permute-start.4 = (f32[1,128]{1,0:T(1,128)S(1)}, f32[1,128]{1,0:T(1,128)S(1)}, u32[]{:S(2)}, u32[]{:S(2)}) collective-permute-start(f32[1,128]{1,0:T(1,128)S(1)} %get-tuple-element.21), channel_id=1, source_target_pairs={{2,0},{4,2},{6,4},{8,6},{10,8},{12,10},{14,12},{16,14},{18,16},{20... | collective-permute-start | bytes 1544 | tf_op jit(solution)/shard_map/ppermute | solution.py:22
  495.1 2.7 collective-permute-start.6
  496.5 4.7 collective-permute-start.7
  501.3 5.6 %collective-permute-start.9 = (f32[1,128]{1,0:T(1,128)S(1)}, f32[1,128]{1,0:T(1,128)S(1)}, u32[]{:S(2)}, u32[]{:S(2)}) collective-permute-start(f32[1,128]{1,0:T(1,128)S(1)} %get-tuple-element.18), channel_id=1, source_target_pairs={{0,2},{2,4},{4,6},{6,8},{8,10},{10,12},{12,14},{14,16},{16,18},{18... | collective-permute-start | bytes 1544 | tf_op jit(solution)/shard_map/ppermute | solution.py:21
  504.9 5.8 %collective-permute-start.8 = (f32[1,128]{1,0:T(1,128)S(1)}, f32[1,128]{1,0:T(1,128)S(1)}, u32[]{:S(2)}, u32[]{:S(2)}) collective-permute-start(f32[1,128]{1,0:T(1,128)S(1)} %get-tuple-element.19), channel_id=1, source_target_pairs={{2,0},{4,2},{6,4},{8,6},{10,8},{12,10},{14,12},{16,14},{18,16},{20... | collective-permute-start | bytes 1544 | tf_op jit(solution)/shard_map/ppermute | solution.py:22
  510.8 3.4 collective-permute-start.10
  512.1 4.7 collective-permute-start.11
where the time goes:
time: 519 us; the launch traced here: 517 us
  local copies, waits for them, and re-layouts  244 us (47%)
  blocking collectives  200 us (39%)
  starting transfers between devices  30 us (6%)
  other arithmetic  18.4 us (4%)
  waiting for transfers between devices  13.7 us (3%)
  matrix products  10.4 us (2%)
    gather x2, local copies, waits for them, and re-layouts, on_device(): nodal = adjoint[:, elem_dofs]  234 us
    psum x2, blocking collectives, apply_dual(): csum = lax.psum(jnp.dot(vec, corners.T, precision=hi), ('gx', 'gy'))  80.5 us
    psum x2, blocking collectives, residual_products(): return lax.psum(inner(resid, zvec), ('gx', 'gy'))  80.2 us
    psum x1, blocking collectives, on_device(): alpha = rz_now / lax.psum(inner(direction, image), ('gx', 'gy'))  38.9 us
    ppermute x6, starting transfers between devices, padded_2(): before = lax.ppermute(last, axis, up)  19.7 us
  transfers between devices with their start and end apart: 12, of which 4 were waited for; matrix products, arithmetic and copies ran while one was open for 2% of the time, Pallas kernels for 0%

commit v1 on v0

--- a/solution.py
+++ b/solution.py
@@ -2,6 +2,7 @@
 import jax.numpy as jnp
 from jax import lax
 from jax.sharding import PartitionSpec as P
+from jax.lax import psum
 
 R = 128
 ITERS = 2
@@ -69,7 +70,7 @@
     rz_now = residual_products(resid, zvec)
     for step in range(ITERS):
         image = apply_dual(direction, op_local, left_idx, right_idx, corners, coarse_inv)
-        alpha = rz_now / lax.psum(inner(direction, image), ("gx", "gy"))
+        alpha = rz_now / psum(psum(inner(direction, image), axis_name="gy"), axis_name="gx")
         adjoint = adjoint + alpha * direction
         resid = resid - alpha * image
         if step + 1 < ITERS:

time: 519 us -> 542 us (1.044)
  blocking collectives: 200 us -> 220 us
    psum x1 -> x4, blocking collectives: 38.9 us -> 58.9 us  [the longest x2 51.1 us: on_device(): psum(psum(inner(direction, image), axis_name='gy'), axis_name='gx')]
where the time goes in v1:
time: 542 us; the launch traced here: 539 us
  local copies, waits for them, and re-layouts  243 us (45%)
  blocking collectives  220 us (41%)
  starting transfers between devices  31.8 us (6%)
  other arithmetic  19.7 us (4%)
  waiting for transfers between devices  13 us (2%)
  matrix products  10.4 us (2%)
    gather x2, local copies, waits for them, and re-layouts, on_device(): nodal = adjoint[:, elem_dofs]  234 us
    psum x2, blocking collectives, residual_products(): return lax.psum(inner(resid, zvec), ('gx', 'gy'))  82.7 us
    psum x2, blocking collectives, apply_dual(): csum = lax.psum(jnp.dot(vec, corners.T, precision=hi), ('gx', 'gy'))  78.6 us
    psum x2, blocking collectives, on_device(): psum(psum(inner(direction, image), axis_name='gy'), axis_name='gx')  51.1 us
    ppermute x6, starting transfers between devices, padded_2(): before = lax.ppermute(last, axis, up)  20.5 us
    ppermute x6, starting transfers between devices, padded_2(): after = lax.ppermute(leading, axis, down)  11.3 us
  transfers between devices with their start and end apart: 12, of which 4 were waited for; matrix products, arithmetic and copies ran while one was open for 2% of the time, Pallas kernels for 0%

profile of v1, /device:TPU:7, one launch (start us, length us, event | category | flops | bytes accessed | tf_op | source)
XLA Modules:
  0.0 539.3 jit_solution(11949246691706915664)
XLA Ops:
  2.5 1.7 bitcast_multiply_fusion.2
  4.2 2.3 gather_fusion
  6.4 3.7 collective-permute-start
  10.1 2.3 gather_fusion.1
  12.4 1.9 collective-permute-start.1
  15.7 39.5 %psum.57 = f32[8,128]{1,0:T(8,128)S(1)} all-reduce(f32[8,128]{1,0:T(8,128)S(1)} %fusion.22), channel_id=1, replica_groups=mesh['gx'=16,'gy'=2] {'gx','gy'}, use_global_device_ids=true, to_apply=%region_2.0 | all-reduce | flops 1024 | bytes 8192 | tf_op jit(solution)/shard_map/psum | solution.py:43
  56.6 1.8 scatter_custom_fusion
  58.4 1.8 scatter_custom_fusion.1
  60.5 3.8 psum.58
  65.0 28.0 %psum.59 = f32[8,1]{0,1:T(1,128)S(1)} all-reduce(f32[8,1]{0,1:T(1,128)S(1)} %psum.58), channel_id=1, replica_groups=mesh['gx'=16,'gy'=2] {'gx'}, use_global_device_ids=true, to_apply=%region_7.0 | all-reduce | flops 8 | bytes 64 | tf_op jit(solution)/shard_map/psum | solution.py:73
  93.0 40.9 %psum.56 = f32[8,1]{0,1:T(1,128)S(1)} all-reduce(f32[8,1]{0,1:T(1,128)S(1)} %bitcast.111), channel_id=1, replica_groups=mesh['gx'=16,'gy'=2] {'gx','gy'}, use_global_device_ids=true, to_apply=%region_1.0 | all-reduce | flops 8 | bytes 64 | tf_op jit(solution)/shard_map/psum | solution.py:53
  134.1 41.8 %psum.60 = f32[8,1]{0,1:T(1,128)S(1)} all-reduce(f32[8,1]{0,1:T(1,128)S(1)} %bitcast.113), channel_id=1, replica_groups=mesh['gx'=16,'gy'=2] {'gx','gy'}, use_global_device_ids=true, to_apply=%region_9.0 | all-reduce | flops 8 | bytes 64 | tf_op jit(solution)/shard_map/psum | solution.py:53
  177.2 2.2 fusion.18
  180.6 39.1 %psum.61 = f32[8,128]{1,0:T(8,128)S(1)} all-reduce(f32[8,128]{1,0:T(8,128)S(1)} %fusion.18), channel_id=1, replica_groups=mesh['gx'=16,'gy'=2] {'gx','gy'}, use_global_device_ids=true, to_apply=%region_10.0 | all-reduce | flops 1024 | bytes 8192 | tf_op jit(solution)/shard_map/psum | solution.py:43
  221.3 6.0 %collective-permute-start.2 = (f32[8,128]{0,1:T(8,128)S(1)}, f32[8,128]{0,1:T(8,128)S(1)}, u32[]{:S(2)}, u32[]{:S(2)}) collective-permute-start(f32[8,128]{0,1:T(8,128)S(1)} %bitcast.116), channel_id=1, source_target_pairs={{0,2},{2,4},{4,6},{6,8},{8,10},{10,12},{12,14},{14,16},{16,18},{18... | collective-permute-start | bytes 12296 | tf_op jit(solution)/shard_map/ppermute | solution.py:22
  227.3 1.9 collective-permute-start.3
  230.9 3.1 scatter_custom_fusion.2
  234.1 3.0 scatter_custom_fusion.3
  238.3 4.0 psum.62
  243.3 23.1 %psum.63 = f32[8,1]{0,1:T(1,128)S(1)} all-reduce(f32[8,1]{0,1:T(1,128)S(1)} %psum.62), channel_id=1, replica_groups=mesh['gx'=16,'gy'=2] {'gx'}, use_global_device_ids=true, to_apply=%region_15.0 | all-reduce | flops 8 | bytes 64 | tf_op jit(solution)/shard_map/psum | solution.py:73
  267.7 215.5 %gather_fusion.4 = f32[65536,8]{1,0:T(8,128)} fusion(f32[8,1024]{0,1:T(8,128)S(1)} %multiply_add_fusion.1, s32[65536]{0:T(1024)S(1)} %broadcast_clamp_fusion), kind=kCustom, calls=%fused_computation.4 | custom fusion | bytes 4456448 | tf_op jit(solution)/shard_map/gather | solution.py:81
  483.2 18.7 %copy.20 = f32[8,64,128,8]{2,0,1,3:T(8,128)} copy(f32[8,64,128,8]{3,2,1,0:T(8,128)} %bitcast.103) | data formatting | bytes 4194304 | tf_op jit(solution)/shard_map/gather | solution.py:81
  501.8 4.2 fusion
  506.1 4.8 collective-permute-start.5
  511.0 1.9 collective-permute-start.4
  512.9 3.8 collective-permute-done.4
  516.8 1.6 collective-permute-start.6
  519.7 3.4 collective-permute-done.7
  523.3 3.4 collective-permute-start.9
  526.7 2.6 collective-permute-start.8
  529.3 3.1 collective-permute-done.8
  535.9 2.6 collective-permute-done.11
  (69 shorter events, 20.8 us)
Async XLA Ops:
  0.6 55.1 %copy-start = (bf16[1,1024,1024]{2,1,0:T(8,128)(2,1)S(1)}, bf16[1,1024,1024]{2,1,0:T(8,128)(2,1)}, u32[]{:S(2)}) copy-start(bf16[1,1024,1024]{2,1,0:T(8,128)(2,1)} %param.11) | copy-start | bytes 6291460
  0.6 14.5 %copy-start.2 = (f32[1,128,1024]{2,1,0:T(8,128)S(1)}, f32[1,128,1024]{2,1,0:T(8,128)}, u32[]{:S(2)}) copy-start(f32[1,128,1024]{2,1,0:T(8,128)} %param.14) | copy-start | bytes 1572868
  0.7 54.5 %copy-start.4 = (f32[128,128]{1,0:T(8,128)S(1)}, f32[128,128]{1,0:T(8,128)}, u32[]{:S(2)}) copy-start(f32[128,128]{1,0:T(8,128)} %param.15) | copy-start | bytes 196612
  1.5 13.6 %copy-start.10 = (s32[128]{0:T(128)}, s32[128]{0:T(128)S(1)}, u32[]{:S(2)}) copy-start(s32[128]{0:T(128)S(1)} %get-tuple-element.21) | copy-start | bytes 1540
  6.4 50.2 %collective-permute-start = (f32[8,128]{0,1:T(8,128)}, f32[8,128]{0,1:T(8,128)}, u32[]{:S(2)}, u32[]{:S(2)}) collective-permute-start(f32[8,128]{0,1:T(8,128)} %bitcast.9), channel_id=1, source_target_pairs={{0,2},{2,4},{4,6},{6,8},{8,10},{10,12},{12,14},{14,16},{16,18},{18... | collective-permute-start | bytes 12296 | tf_op jit(solution)/shard_map/ppermute | solution.py:22
  12.4 46.0 %collective-permute-start.1 = (f32[8,128]{0,1:T(8,128)}, f32[8,128]{0,1:T(8,128)}, u32[]{:S(2)}, u32[]{:S(2)}) collective-permute-start(f32[8,128]{0,1:T(8,128)} %bitcast.11), channel_id=1, source_target_pairs={{2,0},{4,2},{6,4},{8,6},{10,8},{12,10},{14,12},{16,14},{18,16},{20... | collective-permute-start | bytes 12296 | tf_op jit(solution)/shard_map/ppermute | solution.py:23
  55.8 4.5 copy-start.6
  55.8 8.5 %copy-start.5 = (s32[8,64,128]{2,1,0:T(8,128)S(1)}, s32[8,64,128]{2,1,0:T(8,128)}, u32[]{:S(2)}) copy-start(s32[8,64,128]{2,1,0:T(8,128)} %param.17) | copy-start | bytes 786436
  60.2 115.7 %copy-start.3 = (f32[8,1024]{0,1:T(8,128)}, f32[8,1024]{0,1:T(8,128)S(1)}, u32[]{:S(2)}) copy-start(f32[8,1024]{0,1:T(8,128)S(1)} %scatter_custom_fusion.1) | copy-start | bytes 98308
  177.1 59.9 %copy-start.1 = (f32[8,1024]{0,1:T(8,128)}, f32[8,1024]{0,1:T(8,128)S(1)}, u32[]{:S(2)}) copy-start(f32[8,1024]{0,1:T(8,128)S(1)} %multiply_add_fusion) | copy-start | bytes 98308
  221.3 9.6 %collective-permute-start.2 = (f32[8,128]{0,1:T(8,128)S(1)}, f32[8,128]{0,1:T(8,128)S(1)}, u32[]{:S(2)}, u32[]{:S(2)}) collective-permute-start(f32[8,128]{0,1:T(8,128)S(1)} %bitcast.116), channel_id=1, source_target_pairs={{0,2},{2,4},{4,6},{6,8},{8,10},{10,12},{12,14},{14,16},{16,18},{18... | collective-permute-start | bytes 12296 | tf_op jit(solution)/shard_map/ppermute | solution.py:22
  227.3 6.7 %collective-permute-start.3 = (f32[8,128]{0,1:T(8,128)S(1)}, f32[8,128]{0,1:T(8,128)S(1)}, u32[]{:S(2)}, u32[]{:S(2)}) collective-permute-start(f32[8,128]{0,1:T(8,128)S(1)} %bitcast.115), channel_id=1, source_target_pairs={{2,0},{4,2},{6,4},{8,6},{10,8},{12,10},{14,12},{16,14},{18,16},{20... | collective-permute-start | bytes 12296 | tf_op jit(solution)/shard_map/ppermute | solution.py:23
  483.2 18.7 %copy-start.9 = (f32[8,8]{1,0:T(8,128)S(1)}, f32[8,8]{1,0:T(8,128)}, u32[]{:S(2)}) copy-start(f32[8,8]{1,0:T(8,128)} %param.16) | copy-start | bytes 772
  501.8 4.3 copy-start.7
  501.8 4.3 copy-start.8
  506.1 6.8 %collective-permute-start.5 = (f32[1,128]{1,0:T(1,128)S(1)}, f32[1,128]{1,0:T(1,128)S(1)}, u32[]{:S(2)}, u32[]{:S(2)}) collective-permute-start(f32[1,128]{1,0:T(1,128)S(1)} %get-tuple-element.18), channel_id=1, source_target_pairs={{0,2},{2,4},{4,6},{6,8},{8,10},{10,12},{12,14},{14,16},{16,18},{18... | collective-permute-start | bytes 1544 | tf_op jit(solution)/shard_map/ppermute | solution.py:22
  511.0 5.8 %collective-permute-start.4 = (f32[1,128]{1,0:T(1,128)S(1)}, f32[1,128]{1,0:T(1,128)S(1)}, u32[]{:S(2)}, u32[]{:S(2)}) collective-permute-start(f32[1,128]{1,0:T(1,128)S(1)} %get-tuple-element.19), channel_id=1, source_target_pairs={{2,0},{4,2},{6,4},{8,6},{10,8},{12,10},{14,12},{16,14},{18,16},{20... | collective-permute-start | bytes 1544 | tf_op jit(solution)/shard_map/ppermute | solution.py:23
  516.8 2.9 collective-permute-start.6
  518.4 4.7 collective-permute-start.7
  523.3 6.1 %collective-permute-start.9 = (f32[1,128]{1,0:T(1,128)S(1)}, f32[1,128]{1,0:T(1,128)S(1)}, u32[]{:S(2)}, u32[]{:S(2)}) collective-permute-start(f32[1,128]{1,0:T(1,128)S(1)} %get-tuple-element.16), channel_id=1, source_target_pairs={{0,2},{2,4},{4,6},{6,8},{8,10},{10,12},{12,14},{14,16},{16,18},{18... | collective-permute-start | bytes 1544 | tf_op jit(solution)/shard_map/ppermute | solution.py:22
  526.7 5.8 %collective-permute-start.8 = (f32[1,128]{1,0:T(1,128)S(1)}, f32[1,128]{1,0:T(1,128)S(1)}, u32[]{:S(2)}, u32[]{:S(2)}) collective-permute-start(f32[1,128]{1,0:T(1,128)S(1)} %get-tuple-element.17), channel_id=1, source_target_pairs={{2,0},{4,2},{6,4},{8,6},{10,8},{12,10},{14,12},{16,14},{18,16},{20... | collective-permute-start | bytes 1544 | tf_op jit(solution)/shard_map/ppermute | solution.py:23
  532.5 3.4 collective-permute-start.10
  533.9 4.7 collective-permute-start.11
